TPU v7x, 128 devices: a whole 4x4x4 slice. The times are simulated.
128 devices in a mesh: rows: 32 (over x, z, core), ch: 4 (over y).
Axes of the slice: x: 4, y: 4, z: 4, core: 2. Of those that a mesh axis runs over, the one named last changes fastest.
Arguments:
- latent: float32 [4, 64, 160, 512], P(None, 'rows', None, 'ch'), may hold values from -12 to 12
- first_weight: float32 [27, 512, 512], P(None, 'ch'), may hold values from -0.0546875 to 0.0546875
- norm_gain: float32 [512], P('ch'), may hold values from 0.5 to 1.5
- norm_shift: float32 [512], P('ch'), may hold values from -3 to 3
- second_weight: float32 [27, 512, 256], replicated, may hold values from -0.0546875 to 0.0546875
- out_bias: float32 [256], replicated, may hold values from -3 to 3
Outputs:
- decoded: float32 [4, 128, 320, 256], P(None, ('rows', 'ch'))
All inputs are finite; a program needn't handle non-finite values.
Results may differ from a plain program's by a relative error of at most 0.0001.
Values sent between devices are 32-bit elements; how exact they have to be, the bound alone decides.
No kernel may reach another device: no remote copies, remote signals or barrier semaphores. Data moves between devices by JAX's collectives and lax.ppermute only.
A program may use at most 320 MiB of HBM per device.

v0:
```python
import functools
import jax
import jax.numpy as jnp
from jax import lax
from jax.experimental import pallas as pl
from jax.experimental.pallas import tpu as pltpu
from jax.sharding import PartitionSpec as P


EPS = 1e-6
F32 = jnp.float32
BF16 = jnp.bfloat16
T, Q, CB, GW = 4, 160, 128, 16
NR, NC = 32, 4


def split(v):
    hi = v.astype(BF16)
    return hi, (v - hi.astype(F32)).astype(BF16)


def time_inputs(x0, x1, x2, x3):
    return (x0, (x1 + x2) * 0.5, x1 - x0, x1 - x3, x0 - x2, (x2 - x1) * 0.5)


def time_weights(a, b, c):
    ac = a + c
    return (ac + b, c, a, ac - b)


def time_outputs(s0, s1, c0, c1, a, d):
    return (s0, s0 + c0, a + s1 + d, s1 - d - c1)


def shifted(v, by):
    rows = v.shape[0]
    rolled = pltpu.roll(v, by % rows, axis=0)
    q = lax.broadcasted_iota(jnp.int32, v.shape, 0)
    return jnp.where(q == (0 if by > 0 else rows - 1), 0.0, rolled)


def intake(lat, here, head, tail, sems):
    copies = [
        pltpu.make_async_copy(lat, here, sems.at[0]),
        pltpu.make_async_copy(lat.at[:, 0:1], head, sems.at[1]),
        pltpu.make_async_copy(lat.at[:, 1:2], tail, sems.at[2]),
    ]
    for copy in copies:
        copy.start()
    for copy in copies:
        copy.wait()


def fill_row(x, row, get):
    for f, v in enumerate(time_inputs(*(get(t) for t in range(T)))):
        for j in range(3):
            hi, lo = split(v if j == 1 else shifted(v, 1 - j))
            x[f, row, :, j * 256 : j * 256 + 128] = hi
            x[f, row, :, j * 256 + 128 : j * 256 + 256] = lo


def fill_b(w, b):
    def step(k, carry):
        i, j = k // 3, k % 3
        for m, v in enumerate(time_weights(w[k], w[9 + k], w[18 + k])):
            hi, lo = split(v)
            for half in range(2):
                at = pl.ds(pl.multiple_of(j * 256 + half * 128, 128), 128)
                b[m, i, at, 0:128] = hi
                b[m, i, at, 128:256] = lo
        return carry

    lax.fori_loop(0, 9, step, 0)


def products(x, b, p):
    for m, at, n in ((0, 0, 2), (1, 2, 2), (2, 4, 1), (3, 5, 1)):
        total = None
        for i in range(3):
            lhs = x[at : at + n, i : i + 2].reshape(n * 2 * Q, 768)
            term = jnp.dot(lhs, b[m, i], preferred_element_type=F32)
            total = term if total is None else total + term
        p[at : at + n] = halves(total, n)


def halves(v, n):
    return (v[:, :128] + v[:, 128:]).reshape(n, -1, Q, CB)


def local_products(x, b, p):
    for m, at, n in ((0, 0, 2), (1, 2, 2), (2, 4, 1), (3, 5, 1)):
        frames = slice(at, at + n)
        mid = jnp.dot(x[frames, 1:3].reshape(n * 2 * Q, 768), b[m, 1], preferred_element_type=F32)
        p[frames] = halves(mid, n)
        for out_row, in_row, i in ((0, 2, 2), (1, 1, 0)):
            side = jnp.dot(x[frames, in_row].reshape(n * Q, 768), b[m, i], preferred_element_type=F32)
            p[frames, out_row] += halves(side, n)[:, 0]


def edge_products(x, b, before, p):
    for m, at, n in ((0, 0, 2), (1, 2, 2), (2, 4, 1), (3, 5, 1)):
        frames = slice(at, at + n)
        for out_row, in_row, i in ((0, 0, 0), (1, 3, 2)):
            side = jnp.dot(x[frames, in_row].reshape(n * Q, 768), b[m, i], preferred_element_type=F32)
            p[frames, out_row] = before[frames, out_row] + halves(side, n)[:, 0]


def store_chunk(p, lo, hi):
    y = time_outputs(*(p[f] for f in range(6)))
    for t in range(T):
        ref = lo if t < 2 else hi
        ref[t % 2] = y[t]


def conv1_local(ids, lat, w, x, p, b, w1, w2, w3, w0, sems):
    copies = []
    for k, to in enumerate((w0, w1, w2, w3)):
        lanes = pl.ds(pl.multiple_of(ids[k] * CB, CB), CB)
        copies.append(pltpu.make_async_copy(w.at[:, :, lanes], to, sems.at[k]))
        copies[k].start()

    def row(k, carry):
        fill_row(x, k + 1, lambda t: lat[t, k])
        return carry

    lax.fori_loop(0, 2, row, 0)
    copies[0].wait()
    fill_b(w0, b)
    local_products(x, b, p)
    for copy in copies[1:]:
        copy.wait()


def conv1_edge(top, bot, x_in, before, b, lo, hi, x, p):
    fill_row(x, 0, lambda t: top[t, 0])
    fill_row(x, 3, lambda t: bot[t, 0])
    edge_products(x, b, before, p)
    store_chunk(p, lo, hi)


def conv1_more(n, x, *refs):
    b, p = refs[3 * n :]
    for k in range(n):
        fill_b(refs[k], b)
        products(x, b, p)
        store_chunk(p, refs[n + 2 * k], refs[n + 2 * k + 1])


HALF = jax.ShapeDtypeStruct((2, 2, Q, CB), F32)
XS = (6, 4, Q, 768)
BS, PS = (4, 3, 768, 256), (6, 2, Q, CB)
CONV1_SCRATCH = [pltpu.VMEM(BS, BF16), pltpu.VMEM(PS, F32)]
INV = pl.BlockSpec(memory_space=pltpu.VMEM)
INS = pl.BlockSpec(memory_space=pltpu.SMEM)
INH = pl.BlockSpec(memory_space=pltpu.HBM)
MB = 1024 * 1024


def run_intake(lat):
    row = jax.ShapeDtypeStruct((T, 1, Q, CB), F32)
    return pl.pallas_call(
        intake,
        in_specs=[INH],
        out_specs=[INV] * 3,
        scratch_shapes=[pltpu.SemaphoreType.DMA((3,))],
        out_shape=[jax.ShapeDtypeStruct(lat.shape, F32), row, row],
        compiler_params=pltpu.CompilerParams(vmem_limit_bytes=4 * MB),
        cost_estimate=pl.CostEstimate(flops=0, bytes_accessed=2_000_000, transcendentals=0),
        name="intake",
    )(pltpu.with_memory_space_constraint(lat, pltpu.HBM))


def run_conv1_local(ids, lat, w):
    block = jax.ShapeDtypeStruct((27, CB, CB), F32)
    return pl.pallas_call(
        conv1_local,
        in_specs=[INS, INV, INH],
        out_specs=[INV] * 6,
        scratch_shapes=[pltpu.VMEM(block.shape, F32), pltpu.SemaphoreType.DMA((4,))],
        out_shape=[jax.ShapeDtypeStruct(XS, BF16), jax.ShapeDtypeStruct(PS, F32), jax.ShapeDtypeStruct(BS, BF16)]
        + [block] * 3,
        compiler_params=pltpu.CompilerParams(vmem_limit_bytes=10 * MB),
        cost_estimate=pl.CostEstimate(flops=3_000_000_000, bytes_accessed=7_000_000, transcendentals=0),
        name="conv1_local",
    )(ids, lat, pltpu.with_memory_space_constraint(w, pltpu.HBM))


def run_conv1_edge(top, bot, x, before, b):
    return pl.pallas_call(
        conv1_edge,
        in_specs=[INV] * 5,
        out_specs=[INV] * 3,
        scratch_shapes=[pltpu.VMEM(PS, F32)],
        out_shape=[HALF, HALF, jax.ShapeDtypeStruct(XS, BF16)],
        input_output_aliases={2: 2},
        compiler_params=pltpu.CompilerParams(vmem_limit_bytes=10 * MB),
        cost_estimate=pl.CostEstimate(flops=1_500_000_000, bytes_accessed=1_000_000, transcendentals=0),
        name="conv1_edge",
    )(top, bot, x, before, b)


def run_conv1_more(x, *blocks):
    n = len(blocks)
    return pl.pallas_call(
        functools.partial(conv1_more, n),
        in_specs=[INV] * (n + 1),
        out_specs=[INV] * (2 * n),
        scratch_shapes=CONV1_SCRATCH,
        out_shape=[HALF] * (2 * n),
        compiler_params=pltpu.CompilerParams(vmem_limit_bytes=12 * MB),
        cost_estimate=pl.CostEstimate(flops=4_500_000_000 * n, bytes_accessed=2_000_000 * n, transcendentals=0),
        name="conv1_more",
    )(x, *blocks)


def group_sum(v):
    same = (
        lax.broadcasted_iota(jnp.int32, (CB, CB), 0) // GW
        == lax.broadcasted_iota(jnp.int32, (CB, CB), 1) // GW
    ).astype(F32)
    wide = jnp.broadcast_to(v, (8, CB))
    return jnp.dot(wide, same, precision=lax.Precision.HIGHEST, preferred_element_type=F32)[:1]


def finish_first(own_lo, own_hi, a1, a2, b1, b2, gain, shift, even, odd, stats):
    total = jnp.zeros((8, CB), F32)
    for t in range(T):
        own, u, v = (own_lo, a1, a2) if t < 2 else (own_hi, b1, b2)
        for k, out in enumerate((even, odd)):
            y = own[t % 2, k] + u[t % 2, k] + v[t % 2, k]
            out[t] = y
            total = total + y.reshape(Q // 8, 8, CB).sum(0)
    count = float(T * 2 * Q * GW)
    mean = group_sum(total.sum(0, keepdims=True)) / count
    square = jnp.zeros((8, CB), F32)
    for t in range(T):
        for out in (even, odd):
            d = out[t] - mean
            square = square + (d * d).reshape(Q // 8, 8, CB).sum(0)
    m2 = group_sum(square.sum(0, keepdims=True))
    row = jnp.concatenate([mean, m2, gain[...], shift[...]], axis=0)
    stats[...] = jnp.broadcast_to(row[None], stats.shape)


def run_finish(own_lo, own_hi, a1, a2, b1, b2, gain, shift):
    plane = jax.ShapeDtypeStruct((T, Q, CB), F32)
    return pl.pallas_call(
        finish_first,
        out_shape=[plane, plane, jax.ShapeDtypeStruct((NR * NC, 4, CB), F32)],
        in_specs=[INV] * 8,
        out_specs=[INV] * 3,
        compiler_params=pltpu.CompilerParams(vmem_limit_bytes=8 * MB),
        cost_estimate=pl.CostEstimate(flops=2_000_000, bytes_accessed=3_000_000, transcendentals=0),
        name="finish_first",
    )(own_lo, own_hi, a1, a2, b1, b2, gain, shift)


def prep_second(ids, sides, w, out, buf, done, sems):
    def fetch(k):
        at = pl.ds(pl.multiple_of(ids[k] * CB, CB), CB)
        return pltpu.make_async_copy(w.at[:, at, :], buf.at[k % 2], sems.at[k % 2])

    def flush(k):
        return pltpu.make_async_copy(done.at[k % 2], out.at[k], sems.at[2 + k % 2])

    fetch(0).start()
    for block in range(4):
        if block < 3:
            fetch(block + 1).start()
        if block > 1:
            flush(block - 2).wait()
        fetch(block).wait()
        taps_of, to = buf.at[block % 2], done.at[block % 2]

        def build(even_plane):
            def step(k, carry):
                rows = pl.ds(pl.multiple_of(k * 16, 16), 16)
                for side in range(2):
                    taps = []
                    for t in range(3):
                        merged = []
                        for j in range(3):
                            near, mid, far = (taps_of.at[9 * t + 3 * i + j] for i in range(3))
                            if side == 0:
                                g = near[rows, :] if even_plane else near[rows, :] + mid[rows, :]
                            else:
                                g = far[rows, :] + mid[rows, :] if even_plane else far[rows, :]
                            merged.append(g)
                        taps.append((merged[0] + merged[1] + merged[2], merged[0], merged[2]))
                    offset = sides[1 + side] * 128 + k * 16
                    dst = pl.ds(pl.multiple_of(offset, 16), 16)
                    for v in range(3):
                        for m, value in enumerate(time_weights(taps[0][v], taps[1][v], taps[2][v])):
                            hi, lo = split(value)
                            to[m, v, 0, dst, :] = hi
                            to[m, v, 1, dst, :] = lo
                return carry

            lax.fori_loop(0, 8, step, 0)

        @pl.when(sides[0] == 0)
        def _():
            build(True)

        @pl.when(sides[0] == 1)
        def _():
            build(False)

        flush(block).start()
    flush(2).wait()
    flush(3).wait()


W2S = (4, 4, 3, 2, 256, 256)


def run_prep(ids, sides, w):
    return pl.pallas_call(
        prep_second,
        in_specs=[INS, INS, INH],
        out_specs=INH,
        scratch_shapes=[
            pltpu.VMEM((2, 27, CB, 256), F32),
            pltpu.VMEM((2,) + W2S[1:], BF16),
            pltpu.SemaphoreType.DMA((4,)),
        ],
        out_shape=pltpu.HBM(W2S, BF16),
        compiler_params=pltpu.CompilerParams(vmem_limit_bytes=18 * MB),
        cost_estimate=pl.CostEstimate(flops=1_000_000, bytes_accessed=4_000_000, transcendentals=0),
        name="prep_second",
    )(ids, sides, pltpu.with_memory_space_constraint(w, pltpu.HBM))


def norm_silu(ids, k, valid, pair, stats, h):
    block = ids[k]
    count = float(T * 2 * Q * GW)
    means = stats[:, block, 0, :]
    mean = means.sum(0, keepdims=True) / NR
    off = means - mean
    m2 = stats[:, block, 1, :].sum(0, keepdims=True) + count * (off * off).sum(0, keepdims=True)
    scale = stats[0, block, 2:3, :] / jnp.sqrt(m2 / (count * NR) + EPS)
    shift = stats[0, block, 3:4, :]

    def norm(t, carry):
        for side in range(2):
            v = (pair[side][t] - mean) * scale + shift
            v = v / (1.0 + jnp.exp(-v))
            h[t, :, side * 128 : side * 128 + 128] = v * valid[side]
        return carry

    lax.fori_loop(0, T, norm, 0)


def fill_a(h, a):
    def fill(side, carry):
        lanes = pl.ds(pl.multiple_of(side * 128, 128), 128)
        x = time_inputs(*(h[t, :, lanes] for t in range(T)))
        for f in range(6):
            for v, value in enumerate((x[f], shifted(x[f], 1) - x[f], shifted(x[f], -1) - x[f])):
                hi, lo = split(value)
                a[v, 0, f, :, lanes] = hi
                a[v, 1, f, :, lanes] = lo
        return carry

    lax.fori_loop(0, 2, fill, 0)


def multiply_second(a, w, before, acc):
    def multiply(v, carry):
        for m, at, n in ((0, 0, 2), (1, 2, 2), (2, 4, 1), (3, 5, 1)):
            both = a[v, :, at : at + n].reshape(2 * n * Q, 256)
            high = jnp.dot(both, w[m, v, 0], preferred_element_type=F32)
            low = jnp.dot(
                a[v, 0, at : at + n].reshape(n * Q, 256), w[m, v, 1], preferred_element_type=F32
            )
            new = (high[: n * Q] + high[n * Q :] + low).reshape(n, Q, 256)
            acc[v, at : at + n] = new if before is None else before[v, at : at + n] + new
        return carry

    lax.fori_loop(0, 3, multiply, 0)


def conv2_most(ids, valid, e0, o0, e1, o1, e2, o2, stats, w, acc, h, a, wbuf, sems):
    def fetch(k):
        return pltpu.make_async_copy(w.at[k], wbuf.at[k % 2], sems.at[k % 2])

    fetch(0).start()
    for k, pair in enumerate(((e0, o0), (e1, o1), (e2, o2))):
        if k < 2:
            fetch(k + 1).start()
        norm_silu(ids, k, valid, pair, stats, h)
        fill_a(h, a)
        fetch(k).wait()
        multiply_second(a, wbuf.at[k % 2], acc if k else None, acc)


def conv2_last(ids, valid, e3, o3, stats, w, before, bias, out, h, a, wbuf, sems, acc, fine):
    fetch = pltpu.make_async_copy(w.at[3], wbuf.at[0], sems.at[0])
    fetch.start()
    norm_silu(ids, 3, valid, (e3, o3), stats, h)
    fill_a(h, a)
    fetch.wait()
    multiply_second(a, wbuf.at[0], before, acc)
    for half in range(2):
        lanes = slice(half * 128, half * 128 + 128)
        y = time_outputs(*(acc[0, f, :, lanes] for f in range(6)))
        for v in (1, 2):
            z = time_outputs(*(acc[v, f, :, lanes] for f in range(6)))
            for t in range(T):
                fine[t, pl.ds(v - 1, Q, stride=2), :] = y[t] + z[t] + bias[:, lanes]
        out[:, :, lanes] = fine[...]


SUMS = (3, 6, Q, 256)
CONV2_SCRATCH = [
    pltpu.VMEM((T, Q, 256), F32),
    pltpu.VMEM((3, 2, 6, Q, 256), BF16),
    pltpu.VMEM((2,) + W2S[1:], BF16),
    pltpu.SemaphoreType.DMA((2,)),
]


def run_conv2_most(ids, valid, rows, stats, w):
    return pl.pallas_call(
        conv2_most,
        in_specs=[INS, INS] + [INV] * 7 + [INH],
        out_specs=INV,
        scratch_shapes=CONV2_SCRATCH,
        out_shape=jax.ShapeDtypeStruct(SUMS, F32),
        compiler_params=pltpu.CompilerParams(vmem_limit_bytes=14 * MB),
        cost_estimate=pl.CostEstimate(flops=7_000_000_000, bytes_accessed=1_000_000, transcendentals=700_000),
        name="conv2_most",
    )(ids, valid, *rows, stats, pltpu.with_memory_space_constraint(w, pltpu.HBM))


def run_conv2_last(ids, valid, rows, stats, w, before, bias):
    return pl.pallas_call(
        conv2_last,
        in_specs=[INS, INS] + [INV] * 3 + [INH] + [INV] * 2,
        out_specs=INV,
        scratch_shapes=CONV2_SCRATCH + [pltpu.VMEM(SUMS, F32), pltpu.VMEM((T, 2 * Q, 128), F32)],
        out_shape=jax.ShapeDtypeStruct((T, 2 * Q, 256), F32),
        compiler_params=pltpu.CompilerParams(vmem_limit_bytes=18 * MB),
        cost_estimate=pl.CostEstimate(flops=2_300_000_000, bytes_accessed=1_000_000, transcendentals=200_000),
        name="conv2_last",
    )(ids, valid, *rows, stats, pltpu.with_memory_space_constraint(w, pltpu.HBM), before, bias)


def index(r, c):
    return r * NC + c


def holder(r, q, odd):
    if odd and q == 0:
        r += 1
    if not odd and q == 3:
        r -= 1
    return index(r % NR, q)


def row_perm(step, odd, hops):
    pairs = []
    for r in range(NR):
        for p in range(NC):
            a, b = (p + step * (hops - 1)) % NC, (p + step * hops) % NC
            source = index(r, p) if hops == 1 else holder(r, a, odd)
            pairs.append((source, holder(r, b, odd)))
    return pairs


def block(latent, first_weight, norm_gain, norm_shift, second_weight, out_bias):
    c = lax.axis_index("ch")
    r = lax.axis_index("rows")
    both = ("rows", "ch")
    here, head, tail = run_intake(latent)
    top = lax.ppermute(tail, "rows", [(i, i + 1) for i in range(NR - 1)])
    bot = lax.ppermute(head, "rows", [(i + 1, i) for i in range(NR - 1)])

    def ids(*shifts):
        return jnp.stack([(c + s) % NC for s in shifts]).astype(jnp.int32)

    up = [(i, (i + 1) % NC) for i in range(NC)]
    down = [((i + 1) % NC, i) for i in range(NC)]

    def send(v, perm):
        return lax.ppermute(v, "ch", perm)

    x, part, b, w1, w3, w0 = run_conv1_local(ids(2, 1, 3, 0), here, first_weight)
    far_lo, far_hi, x = run_conv1_edge(top, bot, x, part, b)
    got_lo, got_hi = send(far_lo, up), send(far_hi, down)
    up_lo, up_hi, down_lo, down_hi = run_conv1_more(x, w1, w3)
    b1, a1 = send(up_hi, up), send(down_lo, down)
    sum_lo, sum_hi = up_lo + got_lo, down_hi + got_hi
    a2, b2 = send(sum_lo, up), send(sum_hi, down)
    own_lo, own_hi = run_conv1_more(x, w0)

    order = ids(0, 3, 1, 2)
    near = jnp.where((c == 0) | (c == 3), 1, 0)
    sides = jnp.stack([c % 2, near, 1 - near]).astype(jnp.int32)
    tied, _ = lax.optimization_barrier((second_weight, sum_hi))
    w2 = run_prep(order, sides, tied)
    own_lo, w2 = lax.optimization_barrier((own_lo, w2))
    even, odd, stats = run_finish(
        own_lo, own_hi, a1, a2, b1, b2, norm_gain[None], norm_shift[None]
    )

    def move(v, step, is_odd, hops):
        return lax.ppermute(v, both, row_perm(step, is_odd, hops))

    e1, o3 = move(even, 1, False, 1), move(odd, -1, True, 1)
    o1, e3 = move(odd, 1, True, 1), move(even, -1, False, 1)
    edge = [(index(i, 0), index(i + 1, 0)) for i in range(NR - 1)]
    edge += [(index(i + 1, 3), index(i, 3)) for i in range(NR - 1)]
    stats = lax.all_to_all(stats, both, 0, 0, tiled=True).reshape(NR, NC, 4, CB)
    e2, o2 = move(e1, 1, False, 2), move(o3, -1, True, 2)
    halo = lax.ppermute(jnp.where(c == 0, odd, even), both, edge)
    e0, o0 = jnp.where(c == 3, halo, even), jnp.where(c == 0, halo, odd)

    valid = jnp.stack(
        [
            jnp.where((c == 3) & (r == NR - 1), 0.0, 1.0),
            jnp.where((c == 0) & (r == 0), 0.0, 1.0),
        ]
    ).astype(F32)
    sums = run_conv2_most(order, valid, (e0, o0, e1, o1, e3, o3), stats, w2)
    out = run_conv2_last(order, valid, (e2, o2), stats, w2, sums, out_bias[None])
    return out[:, None]


def solution(mesh):
    return jax.shard_map(
        block,
        mesh=mesh,
        in_specs=(P(None, "rows", None, "ch"), P(None, "ch", None), P("ch"), P("ch"), P(), P()),
        out_specs=P(None, ("rows", "ch"), None, None),
        check_vma=False,
    )
```

profile of v0, /device:TPU:1, one launch (start us, length us, event | category | flops | bytes accessed | tf_op | source)
XLA Modules:
  0.0 95.6 jit_solution(3093856408788747148)
XLA Ops:
  0.0 1.3 %intake.1 = (f32[4,2,160,128]{3,2,1,0:T(8,128)S(1)}, f32[4,1,160,128]{3,2,1,0:T(8,128)S(1)}, f32[4,1,160,128]{3,2,1,0:T(8,128)S(1)}) custom-call(f32[4,2,160,128]{3,2,1,0:T(8,128)} %lat.1), custom_call_target="tpu_custom_call" | custom-call | bytes 2000000 | tf_op jit(solution)/shard_map/intake/pallas_call | solution.py:161
  1.4 4.9 %collective-permute-start = (f32[4,1,160,128]{3,2,1,0:T(8,128)S(1)}, f32[4,1,160,128]{3,2,1,0:T(8,128)S(1)}, u32[]{:S(2)}, u32[]{:S(2)}) collective-permute-start(f32[4,1,160,128]{3,2,1,0:T(8,128)S(1)} %get-tuple-element.29), channel_id=1, source_target_pairs={{0,4},{4,8},{8,12},{12,16},{16,20},{20,24},{24,28},{28,32},{32,36}... | collective-permute-start | bytes 983048 | tf_op jit(solution)/shard_map/ppermute | solution.py:476
  6.3 1.9 %collective-permute-start.1 = (f32[4,1,160,128]{3,2,1,0:T(8,128)S(1)}, f32[4,1,160,128]{3,2,1,0:T(8,128)S(1)}, u32[]{:S(2)}, u32[]{:S(2)}) collective-permute-start(f32[4,1,160,128]{3,2,1,0:T(8,128)S(1)} %get-tuple-element.30), channel_id=1, source_target_pairs={{4,0},{8,4},{12,8},{16,12},{20,16},{24,20},{28,24},{32,28},{36,32}... | collective-permute-start | bytes 983048 | tf_op jit(solution)/shard_map/ppermute | solution.py:477
  8.3 0.1 pad_add_fusion
  8.3 0.1 pad_add_fusion.2.sides
  8.4 4.7 %conv1_local.1 = (bf16[6,4,160,768]{3,2,1,0:T(8,128)(2,1)S(1)}, f32[6,2,160,128]{3,2,1,0:T(8,128)S(1)}, bf16[4,3,768,256]{3,2,1,0:T(8,128)(2,1)S(1)}, f32[27,128...) custom-call(s32[4]{0:T(128)S(1)} %get-tuple-element.56.ids, ...), custom_call_target="tpu_custom_call" | custom-call | flops 3000000000 | bytes 7000000 | tf_op jit(solution)/shard_map/conv1_local/pallas_call | solution.py:175
  13.2 1.8 %collective-permute-done.1.bot = f32[4,1,160,128]{3,2,1,0:T(8,128)S(1)} collective-permute-done((f32[4,1,160,128]{3,2,1,0:T(8,128)S(1)}, f32[4,1,160,128]{3,2,1,0:T(8,128)S(1)}, u32[]{:S(2)}, u32[]{:S(2)}) %collective-permute-start.1) | collective-permute-done | bytes 327712 | tf_op jit(solution)/shard_map/ppermute | solution.py:477
  15.0 1.1 %conv1_edge.1 = (f32[2,2,160,128]{3,2,1,0:T(8,128)S(1)}, f32[2,2,160,128]{3,2,1,0:T(8,128)S(1)}, bf16[6,4,160,768]{3,2,1,0:T(8,128)(2,1)S(1)}) custom-call(f32[4,1,160,128]{3,2,1,0:T(8,128)S(1)} %collective-permute-done.top, f32[4,1,160,128]{3,2,1,0:T(8,128)S(1)} %collective-permute-done.1.bot, ...), custom_call_target="tpu_custom_call", output_to_operand_aliasing={{2}: (2, {})} | custom-call | flops 1500000000 | bytes 1000000 | tf_op jit(solution)/shard_map/conv1_edge/pallas_call | solution.py:189
  16.1 2.5 %collective-permute-start.2 = (f32[2,2,160,128]{3,2,1,0:T(8,128)S(1)}, f32[2,2,160,128]{3,2,1,0:T(8,128)S(1)}, u32[]{:S(2)}, u32[]{:S(2)}) collective-permute-start(f32[2,2,160,128]{3,2,1,0:T(8,128)S(1)} %get-tuple-element.41), channel_id=1, source_target_pairs={{1,0},{2,1},{3,2},{0,3},{5,4},{6,5},{7,6},{4,7},{9,8},{10,9},{11,1... | collective-permute-start | bytes 983048 | tf_op jit(solution)/shard_map/ppermute | solution.py:486
  18.6 0.0 collective-permute-start.4
  18.6 6.8 %conv1_more.3 = (f32[2,2,160,128]{3,2,1,0:T(8,128)S(1)}, f32[2,2,160,128]{3,2,1,0:T(8,128)S(1)}, f32[2,2,160,128]{3,2,1,0:T(8,128)S(1)}, f32[2,2,160,128]{3,2,1,0:T(8,128)S(1)}) custom-call(bf16[6,4,160,768]{3,2,1,0:T(8,128)(2,1)S(1)} %get-tuple-element.35.x, f32[27,128,128]{2,1,0:T(8,128)S(1)} %get-tuple-element.38.refs_0_, ...), custom_call_target="tpu_custom_call" | custom-call | flops 8999999488 | bytes 4000000 | tf_op jit(solution)/shard_map/conv1_more/pallas_call | solution.py:204
  25.4 2.7 %collective-permute-start.3 = (f32[2,2,160,128]{3,2,1,0:T(8,128)S(1)}, f32[2,2,160,128]{3,2,1,0:T(8,128)S(1)}, u32[]{:S(2)}, u32[]{:S(2)}) collective-permute-start(f32[2,2,160,128]{3,2,1,0:T(8,128)S(1)} %get-tuple-element.45), channel_id=1, source_target_pairs={{1,0},{2,1},{3,2},{0,3},{5,4},{6,5},{7,6},{4,7},{9,8},{10,9},{11,1... | collective-permute-start | bytes 983048 | tf_op jit(solution)/shard_map/ppermute | solution.py:486
  28.2 2.7 %collective-permute-start.7 = (f32[2,2,160,128]{3,2,1,0:T(8,128)S(1)}, f32[2,2,160,128]{3,2,1,0:T(8,128)S(1)}, u32[]{:S(2)}, u32[]{:S(2)}) collective-permute-start(f32[2,2,160,128]{3,2,1,0:T(8,128)S(1)} %add.46), channel_id=1, source_target_pairs={{1,0},{2,1},{3,2},{0,3},{5,4},{6,5},{7,6},{4,7},{9,8},{10,9},{11,1... | collective-permute-start | bytes 983048 | tf_op jit(solution)/shard_map/ppermute | solution.py:486
  31.0 0.1 add.47
  31.0 0.1 collective-permute-start.5
  31.1 3.4 %conv1_more.2 = (f32[2,2,160,128]{3,2,1,0:T(8,128)S(1)}, f32[2,2,160,128]{3,2,1,0:T(8,128)S(1)}) custom-call(bf16[6,4,160,768]{3,2,1,0:T(8,128)(2,1)S(1)} %get-tuple-element.35.x, f32[27,128,128]{2,1,0:T(8,128)S(1)} %get-tuple-element.36.refs_0_), custom_call_target="tpu_custom_call" | custom-call | flops 4499999744 | bytes 2000000 | tf_op jit(solution)/shard_map/conv1_more/pallas_call | solution.py:204
  34.5 0.0 copy-start.1
  34.5 0.0 copy-start.2
  34.5 10.8 %prep_second.1.w = bf16[4,4,3,2,256,256]{5,4,3,2,1,0:T(8,128)(2,1)} custom-call(s32[4]{0:T(128)S(1)} %get-tuple-element.55.ids, s32[3]{0:T(128)S(1)} %pad_add_fusion.2.sides, f32[27,512,256]{2,1,0:T(8,128)} %w.2), custom_call_target="tpu_custom_call" | custom-call | flops 1000000 | bytes 4000000 | tf_op jit(solution)/shard_map/prep_second/pallas_call | solution.py:318
  45.4 1.4 %finish_first.1 = (f32[4,160,128]{2,1,0:T(8,128)S(1)}, f32[4,160,128]{2,1,0:T(8,128)S(1)}, f32[128,4,128]{2,1,0:T(4,128)}) custom-call(f32[2,2,160,128]{3,2,1,0:T(8,128)S(1)} %get-tuple-element.43.own_lo, f32[2,2,160,128]{3,2,1,0:T(8,128)S(1)} %get-tuple-element.44.own_hi, f32[2,2,160,128]{3,2,1,0:T(8,128)S(1)} %collective-permute-done.3.a1, ...), custom_call_target="tpu_custom_call" | custom-call | flops 2000000 | bytes 3000000 | tf_op jit(solution)/shard_map/finish_first/pallas_call | solution.py:247
  46.8 2.7 %collective-permute-start.10 = (f32[4,160,128]{2,1,0:T(8,128)S(1)}, f32[4,160,128]{2,1,0:T(8,128)S(1)}, u32[]{:S(2)}, u32[]{:S(2)}) collective-permute-start(f32[4,160,128]{2,1,0:T(8,128)S(1)} %get-tuple-element.50), channel_id=1, source_target_pairs={{0,3},{1,4},{2,1},{3,2},{4,7},{5,8},{6,5},{7,6},{8,11},{9,12},{10,... | collective-permute-start | bytes 983048 | tf_op jit(solution)/shard_map/ppermute | solution.py:508
  49.5 5.1 %collective-permute-start.12 = (f32[4,160,128]{2,1,0:T(8,128)S(1)}, f32[4,160,128]{2,1,0:T(8,128)}, u32[]{:S(2)}, u32[]{:S(2)}) collective-permute-start(f32[4,160,128]{2,1,0:T(8,128)S(1)} %broadcast_select_fusion.1), channel_id=1, source_target_pairs={{0,4},{4,8},{8,12},{12,16},{16,20},{20,24},{24,28},{28,32},{32,36}... | collective-permute-start | bytes 983048 | tf_op jit(solution)/shard_map/ppermute | solution.py:516
  54.6 0.9 collective-permute-start.14
  55.5 0.6 collective-permute-start.13
  56.2 0.1 pad_maximum_fusion.valid
  56.2 11.7 %all-to-all-start = ((f32[128,4,128]{2,1,0:T(4,128)}), f32[128,4,128]{2,1,0:T(4,128)S(1)}, u32[]{:S(2)}, u32[]{:S(2)}) async-start(f32[128,4,128]{2,1,0:T(4,128)} %get-tuple-element.51), calls=%async_computation | async-start | bytes 524288 | tf_op jit(solution)/shard_map/all_to_all | solution.py:514
  68.0 1.4 %collective-permute-start.9 = (f32[4,160,128]{2,1,0:T(8,128)S(1)}, f32[4,160,128]{2,1,0:T(8,128)S(1)}, u32[]{:S(2)}, u32[]{:S(2)}) collective-permute-start(f32[4,160,128]{2,1,0:T(8,128)S(1)} %collective-permute-done.8.e1), channel_id=1, source_target_pairs={{1,2},{2,127},{127,0},{0,1},{5,6},{6,3},{3,4},{4,5},{9,10},{10,7},... | collective-permute-start | bytes 983048 | tf_op jit(solution)/shard_map/ppermute | solution.py:508
  69.4 1.6 %collective-permute-start.11 = (f32[4,160,128]{2,1,0:T(8,128)S(1)}, f32[4,160,128]{2,1,0:T(8,128)S(1)}, u32[]{:S(2)}, u32[]{:S(2)}) collective-permute-start(f32[4,160,128]{2,1,0:T(8,128)S(1)} %collective-permute-done.10.o2), channel_id=1, source_target_pairs={{3,2},{4,3},{1,4},{2,1},{7,6},{8,7},{5,8},{6,5},{11,10},{12,11},{9... | collective-permute-start | bytes 983048 | tf_op jit(solution)/shard_map/ppermute | solution.py:508
  71.1 1.0 %broadcast_select_fusion = (f32[4,160,128]{2,1,0:T(8,128)S(1)}, f32[4,160,128]{2,1,0:T(8,128)S(1)}) fusion(f32[4,160,128]{2,1,0:T(8,128)} %collective-permute-done.12, f32[4,160,128]{2,1,0:T(8,128)S(1)} %get-tuple-element.50, pred[]{:T(512)S(6)} %eq.29, f32[4,160,128]{2,1,0:T(8,128)S(1)} %get-tuple-element.49, pred[]{:T(512)S(6)} %eq.27), kind=kLoop, calls=%fused_computation | loop fusion | flops 163840 | bytes 1638402 | tf_op jit(solution)/shard_map/jit(_where)/select_n | solution.py:517
  72.1 8.1 %all-to-all-done = f32[128,4,128]{2,1,0:T(4,128)S(1)} async-done(((f32[128,4,128]{2,1,0:T(4,128)}), f32[128,4,128]{2,1,0:T(4,128)S(1)}, u32[]{:S(2)}, u32[]{:S(2)}) %all-to-all-start) | async-done | bytes 262176 | tf_op jit(solution)/shard_map/all_to_all | solution.py:514
  80.3 9.5 %conv2_most.1.before = f32[3,6,160,256]{3,2,1,0:T(8,128)S(1)} custom-call(s32[4]{0:T(128)S(1)} %get-tuple-element.55.ids, f32[2]{0:T(128)S(1)} %pad_maximum_fusion.valid, f32[4,160,128]{2,1,0:T(8,128)S(1)} %get-tuple-element.54.e0, f32[4,160,128]{2,1,0:T(8,128)S(1)} %get-tuple-element.53.o0, f32[4,160,128]{2,1,0:T(8,128)S(1)} %collective-permute-done.8.e1, ...), custom_call_target="tpu_custom_call" | custom-call | flops 7000000000 | bytes 1000000 | tf_op jit(solution)/shard_map/conv2_most/pallas_call | solution.py:424
  89.8 5.6 %conv2_last.1 = f32[4,320,256]{2,1,0:T(8,128)} custom-call(s32[4]{0:T(128)S(1)} %get-tuple-element.55.ids, f32[2]{0:T(128)S(1)} %pad_maximum_fusion.valid, f32[4,160,128]{2,1,0:T(8,128)S(1)} %collective-permute-done.9.e3, f32[4,160,128]{2,1,0:T(8,128)S(1)} %collective-permute-done.11.o3, f32[32,4,4,128]{3,2,1,0:T(4,128)S(1)} %bitcast.17, ...), custom_call_target="tpu_custom_call" | custom-call | flops 2300000000 | bytes 1000000 | tf_op jit(solution)/shard_map/conv2_last/pallas_call | solution.py:437
  (22 shorter events, 0.1 us)
Async XLA Ops:
  1.4 11.8 %collective-permute-start = (f32[4,1,160,128]{3,2,1,0:T(8,128)S(1)}, f32[4,1,160,128]{3,2,1,0:T(8,128)S(1)}, u32[]{:S(2)}, u32[]{:S(2)}) collective-permute-start(f32[4,1,160,128]{3,2,1,0:T(8,128)S(1)} %get-tuple-element.29), channel_id=1, source_target_pairs={{0,4},{4,8},{8,12},{12,16},{16,20},{20,24},{24,28},{28,32},{32,36}... | collective-permute-start | bytes 983048 | tf_op jit(solution)/shard_map/ppermute | solution.py:476
  6.3 8.7 %collective-permute-start.1 = (f32[4,1,160,128]{3,2,1,0:T(8,128)S(1)}, f32[4,1,160,128]{3,2,1,0:T(8,128)S(1)}, u32[]{:S(2)}, u32[]{:S(2)}) collective-permute-start(f32[4,1,160,128]{3,2,1,0:T(8,128)S(1)} %get-tuple-element.30), channel_id=1, source_target_pairs={{4,0},{8,4},{12,8},{16,12},{20,16},{24,20},{28,24},{32,28},{36,32}... | collective-permute-start | bytes 983048 | tf_op jit(solution)/shard_map/ppermute | solution.py:477
  16.1 12.1 %collective-permute-start.2 = (f32[2,2,160,128]{3,2,1,0:T(8,128)S(1)}, f32[2,2,160,128]{3,2,1,0:T(8,128)S(1)}, u32[]{:S(2)}, u32[]{:S(2)}) collective-permute-start(f32[2,2,160,128]{3,2,1,0:T(8,128)S(1)} %get-tuple-element.41), channel_id=1, source_target_pairs={{1,0},{2,1},{3,2},{0,3},{5,4},{6,5},{7,6},{4,7},{9,8},{10,9},{11,1... | collective-permute-start | bytes 983048 | tf_op jit(solution)/shard_map/ppermute | solution.py:486
  18.6 12.4 %collective-permute-start.4 = (f32[2,2,160,128]{3,2,1,0:T(8,128)S(1)}, f32[2,2,160,128]{3,2,1,0:T(8,128)S(1)}, u32[]{:S(2)}, u32[]{:S(2)}) collective-permute-start(f32[2,2,160,128]{3,2,1,0:T(8,128)S(1)} %get-tuple-element.47), channel_id=1, source_target_pairs={{0,1},{1,2},{2,3},{3,0},{4,5},{5,6},{6,7},{7,4},{8,9},{9,10},{10,1... | collective-permute-start | bytes 983048 | tf_op jit(solution)/shard_map/ppermute | solution.py:486
  25.4 19.9 %collective-permute-start.3 = (f32[2,2,160,128]{3,2,1,0:T(8,128)S(1)}, f32[2,2,160,128]{3,2,1,0:T(8,128)S(1)}, u32[]{:S(2)}, u32[]{:S(2)}) collective-permute-start(f32[2,2,160,128]{3,2,1,0:T(8,128)S(1)} %get-tuple-element.45), channel_id=1, source_target_pairs={{1,0},{2,1},{3,2},{0,3},{5,4},{6,5},{7,6},{4,7},{9,8},{10,9},{11,1... | collective-permute-start | bytes 983048 | tf_op jit(solution)/shard_map/ppermute | solution.py:486
  28.2 17.2 %collective-permute-start.6 = (f32[2,2,160,128]{3,2,1,0:T(8,128)S(1)}, f32[2,2,160,128]{3,2,1,0:T(8,128)S(1)}, u32[]{:S(2)}, u32[]{:S(2)}) collective-permute-start(f32[2,2,160,128]{3,2,1,0:T(8,128)S(1)} %get-tuple-element.48), channel_id=1, source_target_pairs={{0,1},{1,2},{2,3},{3,0},{4,5},{5,6},{6,7},{7,4},{8,9},{9,10},{10,1... | collective-permute-start | bytes 983048 | tf_op jit(solution)/shard_map/ppermute | solution.py:486
  28.2 17.1 %collective-permute-start.7 = (f32[2,2,160,128]{3,2,1,0:T(8,128)S(1)}, f32[2,2,160,128]{3,2,1,0:T(8,128)S(1)}, u32[]{:S(2)}, u32[]{:S(2)}) collective-permute-start(f32[2,2,160,128]{3,2,1,0:T(8,128)S(1)} %add.46), channel_id=1, source_target_pairs={{1,0},{2,1},{3,2},{0,3},{5,4},{6,5},{7,6},{4,7},{9,8},{10,9},{11,1... | collective-permute-start | bytes 983048 | tf_op jit(solution)/shard_map/ppermute | solution.py:486
  31.0 14.3 %collective-permute-start.5 = (f32[2,2,160,128]{3,2,1,0:T(8,128)S(1)}, f32[2,2,160,128]{3,2,1,0:T(8,128)S(1)}, u32[]{:S(2)}, u32[]{:S(2)}) collective-permute-start(f32[2,2,160,128]{3,2,1,0:T(8,128)S(1)} %add.47), channel_id=1, source_target_pairs={{0,1},{1,2},{2,3},{3,0},{4,5},{5,6},{6,7},{7,4},{8,9},{9,10},{10,1... | collective-permute-start | bytes 983048 | tf_op jit(solution)/shard_map/ppermute | solution.py:486
  34.5 10.8 %copy-start.1 = (f32[128]{0:T(128)S(1)}, f32[128]{0:T(128)}, u32[]{:S(2)}) copy-start(f32[128]{0:T(128)} %param.8) | copy-start | bytes 1540
  34.5 10.8 %copy-start.2 = (f32[128]{0:T(128)S(1)}, f32[128]{0:T(128)}, u32[]{:S(2)}) copy-start(f32[128]{0:T(128)} %param.9) | copy-start | bytes 1540
  46.8 21.2 %collective-permute-start.8 = (f32[4,160,128]{2,1,0:T(8,128)S(1)}, f32[4,160,128]{2,1,0:T(8,128)S(1)}, u32[]{:S(2)}, u32[]{:S(2)}) collective-permute-start(f32[4,160,128]{2,1,0:T(8,128)S(1)} %get-tuple-element.49), channel_id=1, source_target_pairs={{0,1},{1,2},{2,127},{3,0},{4,5},{5,6},{6,3},{7,4},{8,9},{9,10},{10... | collective-permute-start | bytes 983048 | tf_op jit(solution)/shard_map/ppermute | solution.py:508
  46.8 22.7 %collective-permute-start.10 = (f32[4,160,128]{2,1,0:T(8,128)S(1)}, f32[4,160,128]{2,1,0:T(8,128)S(1)}, u32[]{:S(2)}, u32[]{:S(2)}) collective-permute-start(f32[4,160,128]{2,1,0:T(8,128)S(1)} %get-tuple-element.50), channel_id=1, source_target_pairs={{0,3},{1,4},{2,1},{3,2},{4,7},{5,8},{6,5},{7,6},{8,11},{9,12},{10,... | collective-permute-start | bytes 983048 | tf_op jit(solution)/shard_map/ppermute | solution.py:508
  49.5 21.6 %collective-permute-start.12 = (f32[4,160,128]{2,1,0:T(8,128)S(1)}, f32[4,160,128]{2,1,0:T(8,128)}, u32[]{:S(2)}, u32[]{:S(2)}) collective-permute-start(f32[4,160,128]{2,1,0:T(8,128)S(1)} %broadcast_select_fusion.1), channel_id=1, source_target_pairs={{0,4},{4,8},{8,12},{12,16},{16,20},{20,24},{24,28},{28,32},{32,36}... | collective-permute-start | bytes 983048 | tf_op jit(solution)/shard_map/ppermute | solution.py:516
  54.6 25.6 %collective-permute-start.14 = (f32[4,160,128]{2,1,0:T(8,128)S(1)}, f32[4,160,128]{2,1,0:T(8,128)S(1)}, u32[]{:S(2)}, u32[]{:S(2)}) collective-permute-start(f32[4,160,128]{2,1,0:T(8,128)S(1)} %get-tuple-element.49), channel_id=1, source_target_pairs={{0,127},{1,0},{2,1},{3,2},{4,3},{5,4},{6,5},{7,6},{8,7},{9,8},{10,... | collective-permute-start | bytes 983048 | tf_op jit(solution)/shard_map/ppermute | solution.py:508
  55.5 24.7 %collective-permute-start.13 = (f32[4,160,128]{2,1,0:T(8,128)S(1)}, f32[4,160,128]{2,1,0:T(8,128)S(1)}, u32[]{:S(2)}, u32[]{:S(2)}) collective-permute-start(f32[4,160,128]{2,1,0:T(8,128)S(1)} %get-tuple-element.50), channel_id=1, source_target_pairs={{0,1},{1,2},{2,3},{3,4},{4,5},{5,6},{6,7},{7,8},{8,9},{9,10},{10,1... | collective-permute-start | bytes 983048 | tf_op jit(solution)/shard_map/ppermute | solution.py:508
  56.2 24.0 %all-to-all-start = ((f32[128,4,128]{2,1,0:T(4,128)}), f32[128,4,128]{2,1,0:T(4,128)S(1)}, u32[]{:S(2)}, u32[]{:S(2)}) async-start(f32[128,4,128]{2,1,0:T(4,128)} %get-tuple-element.51), calls=%async_computation | async-start | bytes 524288 | tf_op jit(solution)/shard_map/all_to_all | solution.py:514
  68.0 21.8 %collective-permute-start.9 = (f32[4,160,128]{2,1,0:T(8,128)S(1)}, f32[4,160,128]{2,1,0:T(8,128)S(1)}, u32[]{:S(2)}, u32[]{:S(2)}) collective-permute-start(f32[4,160,128]{2,1,0:T(8,128)S(1)} %collective-permute-done.8.e1), channel_id=1, source_target_pairs={{1,2},{2,127},{127,0},{0,1},{5,6},{6,3},{3,4},{4,5},{9,10},{10,7},... | collective-permute-start | bytes 983048 | tf_op jit(solution)/shard_map/ppermute | solution.py:508
  69.4 20.3 %collective-permute-start.11 = (f32[4,160,128]{2,1,0:T(8,128)S(1)}, f32[4,160,128]{2,1,0:T(8,128)S(1)}, u32[]{:S(2)}, u32[]{:S(2)}) collective-permute-start(f32[4,160,128]{2,1,0:T(8,128)S(1)} %collective-permute-done.10.o2), channel_id=1, source_target_pairs={{3,2},{4,3},{1,4},{2,1},{7,6},{8,7},{5,8},{6,5},{11,10},{12,11},{9... | collective-permute-start | bytes 983048 | tf_op jit(solution)/shard_map/ppermute | solution.py:508
  80.2 9.5 %copy-start = (f32[256]{0:T(256)S(1)}, f32[256]{0:T(256)}, u32[]{:S(2)}) copy-start(f32[256]{0:T(256)} %param.11) | copy-start | bytes 3076
where the time goes:
time: 95.9 us; the launch traced here: 95.6 us
  Pallas kernels  44.7 us (47%)
  starting transfers between devices  39.1 us (41%)
  waiting for transfers between devices  9.97 us (10%)
  other arithmetic  1.38 us (1%)
    all_to_all x1, starting transfers between devices, block(): stats = lax.all_to_all(stats, both, 0, 0, tiled=True).reshape(NR, NC, 4, CB)  11.7 us
    pallas_call x1, Pallas kernels, run_prep(): pl.pallas_call(prep_second, in_specs=[INS, INS, INH], out_specs=INH, scra...  10.8 us
    pallas_call x2, Pallas kernels, run_conv1_more(): pl.pallas_call(functools.partial(conv1_more, n), in_specs=[INV] * (n + 1)...  10.3 us
    pallas_call x1, Pallas kernels, run_conv2_most(): pl.pallas_call(conv2_most, in_specs=[INS, INS] + [INV] * 7 + [INH], out_s...  9.5 us
    all_to_all x1, waiting for transfers between devices, block(): stats = lax.all_to_all(stats, both, 0, 0, tiled=True).reshape(NR, NC, 4, CB)  8.14 us
    ppermute x6, starting transfers between devices, send(): return lax.ppermute(v, 'ch', perm)  8.07 us
    ppermute x6, starting transfers between devices, move(): return lax.ppermute(v, both, row_perm(step, is_odd, hops))  7.28 us
    pallas_call x1, Pallas kernels, run_conv2_last(): pl.pallas_call(conv2_last, in_specs=[INS, INS] + [INV] * 3 + [INH] + [INV...  5.64 us
  transfers between devices with their start and end apart: 16, of which 2 were waited for; matrix products, arithmetic and copies ran while one was open for 1% of the time, Pallas kernels for 37%

commit v1 on v0

--- a/solution.py
+++ b/solution.py
@@ -146,6 +146,18 @@
         store_chunk(p, refs[n + 2 * k], refs[n + 2 * k + 1])
 
 
+def conv1_near(ids, x, w1, w3, w2, *refs):
+    outs, taps, (b, p, sems) = refs[:4], refs[4:8], refs[8:]
+    copies = []
+    for k in range(4):
+        at = pl.ds(pl.multiple_of(ids[k] * CB, CB), CB)
+        copies.append(pltpu.make_async_copy(w2.at[:, at, :], taps[k], sems.at[k]))
+        copies[k].start()
+    conv1_more(2, x, w1, w3, *outs, b, p)
+    for copy in copies:
+        copy.wait()
+
+
 HALF = jax.ShapeDtypeStruct((2, 2, Q, CB), F32)
 XS = (6, 4, Q, 768)
 BS, PS = (4, 3, 768, 256), (6, 2, Q, CB)
@@ -207,10 +219,23 @@
         out_specs=[INV] * (2 * n),
         scratch_shapes=CONV1_SCRATCH,
         out_shape=[HALF] * (2 * n),
-        compiler_params=pltpu.CompilerParams(vmem_limit_bytes=12 * MB),
+        compiler_params=pltpu.CompilerParams(vmem_limit_bytes=10 * MB),
         cost_estimate=pl.CostEstimate(flops=4_500_000_000 * n, bytes_accessed=2_000_000 * n, transcendentals=0),
         name="conv1_more",
     )(x, *blocks)
+
+
+def run_conv1_near(ids, x, w1, w3, w2):
+    return pl.pallas_call(
+        conv1_near,
+        in_specs=[INS] + [INV] * 3 + [INH],
+        out_specs=[INV] * 8,
+        scratch_shapes=CONV1_SCRATCH + [pltpu.SemaphoreType.DMA((4,))],
+        out_shape=[HALF] * 4 + [jax.ShapeDtypeStruct((27, CB, 256), F32)] * 4,
+        compiler_params=pltpu.CompilerParams(vmem_limit_bytes=10 * MB),
+        cost_estimate=pl.CostEstimate(flops=9_000_000_000, bytes_accessed=16_000_000, transcendentals=0),
+        name="conv1_near",
+    )(ids, x, w1, w3, pltpu.with_memory_space_constraint(w2, pltpu.HBM))
 
 
 def group_sum(v):
@@ -222,7 +247,7 @@
     return jnp.dot(wide, same, precision=lax.Precision.HIGHEST, preferred_element_type=F32)[:1]
 
 
-def finish_first(own_lo, own_hi, a1, a2, b1, b2, gain, shift, even, odd, stats):
+def finish_first(plane, own_lo, own_hi, a1, a2, b1, b2, gain, shift, even, odd, edge, stats):
     total = jnp.zeros((8, CB), F32)
     for t in range(T):
         own, u, v = (own_lo, a1, a2) if t < 2 else (own_hi, b1, b2)
@@ -234,6 +259,7 @@
     mean = group_sum(total.sum(0, keepdims=True)) / count
     square = jnp.zeros((8, CB), F32)
     for t in range(T):
+        edge[t] = jnp.where(plane[0] == 0, odd[t], even[t])
         for out in (even, odd):
             d = out[t] - mean
             square = square + (d * d).reshape(Q // 8, 8, CB).sum(0)
@@ -242,35 +268,29 @@
     stats[...] = jnp.broadcast_to(row[None], stats.shape)
 
 
-def run_finish(own_lo, own_hi, a1, a2, b1, b2, gain, shift):
+def run_finish(plane_id, own_lo, own_hi, a1, a2, b1, b2, gain, shift):
     plane = jax.ShapeDtypeStruct((T, Q, CB), F32)
     return pl.pallas_call(
         finish_first,
-        out_shape=[plane, plane, jax.ShapeDtypeStruct((NR * NC, 4, CB), F32)],
-        in_specs=[INV] * 8,
-        out_specs=[INV] * 3,
+        out_shape=[plane, plane, plane, jax.ShapeDtypeStruct((NR * NC, 4, CB), F32)],
+        in_specs=[INS] + [INV] * 8,
+        out_specs=[INV] * 4,
         compiler_params=pltpu.CompilerParams(vmem_limit_bytes=8 * MB),
         cost_estimate=pl.CostEstimate(flops=2_000_000, bytes_accessed=3_000_000, transcendentals=0),
         name="finish_first",
-    )(own_lo, own_hi, a1, a2, b1, b2, gain, shift)
-
-
-def prep_second(ids, sides, w, out, buf, done, sems):
-    def fetch(k):
-        at = pl.ds(pl.multiple_of(ids[k] * CB, CB), CB)
-        return pltpu.make_async_copy(w.at[:, at, :], buf.at[k % 2], sems.at[k % 2])
+    )(plane_id, own_lo, own_hi, a1, a2, b1, b2, gain, shift)
+
+
+def prep_second(sides, *refs):
+    blocks, (out, done, sems) = refs[:4], refs[4:]
 
     def flush(k):
-        return pltpu.make_async_copy(done.at[k % 2], out.at[k], sems.at[2 + k % 2])
-
-    fetch(0).start()
+        return pltpu.make_async_copy(done.at[k % 2], out.at[k], sems.at[k % 2])
+
     for block in range(4):
-        if block < 3:
-            fetch(block + 1).start()
         if block > 1:
             flush(block - 2).wait()
-        fetch(block).wait()
-        taps_of, to = buf.at[block % 2], done.at[block % 2]
+        taps_of, to = blocks[block], done.at[block % 2]
 
         def build(even_plane):
             def step(k, carry):
@@ -314,21 +334,21 @@
 W2S = (4, 4, 3, 2, 256, 256)
 
 
-def run_prep(ids, sides, w):
+def run_prep(sides, blocks):
     return pl.pallas_call(
         prep_second,
-        in_specs=[INS, INS, INH],
+        in_specs=[INS] + [INV] * 4,
         out_specs=INH,
-        scratch_shapes=[
-            pltpu.VMEM((2, 27, CB, 256), F32),
-            pltpu.VMEM((2,) + W2S[1:], BF16),
-            pltpu.SemaphoreType.DMA((4,)),
-        ],
+        scratch_shapes=[pltpu.VMEM((2,) + W2S[1:], BF16), pltpu.SemaphoreType.DMA((2,))],
         out_shape=pltpu.HBM(W2S, BF16),
-        compiler_params=pltpu.CompilerParams(vmem_limit_bytes=18 * MB),
+        compiler_params=pltpu.CompilerParams(vmem_limit_bytes=10 * MB),
         cost_estimate=pl.CostEstimate(flops=1_000_000, bytes_accessed=4_000_000, transcendentals=0),
         name="prep_second",
-    )(ids, sides, pltpu.with_memory_space_constraint(w, pltpu.HBM))
+    )(sides, *blocks)
+
+
+def rows_of(even, odd):
+    return lambda t: even[t], lambda t: odd[t]
 
 
 def norm_silu(ids, k, valid, pair, stats, h):
@@ -343,7 +363,7 @@
 
     def norm(t, carry):
         for side in range(2):
-            v = (pair[side][t] - mean) * scale + shift
+            v = (pair[side](t) - mean) * scale + shift
             v = v / (1.0 + jnp.exp(-v))
             h[t, :, side * 128 : side * 128 + 128] = v * valid[side]
         return carry
@@ -366,84 +386,85 @@
 
 
 def multiply_second(a, w, before, acc):
-    def multiply(v, carry):
+    for v in range(3):
         for m, at, n in ((0, 0, 2), (1, 2, 2), (2, 4, 1), (3, 5, 1)):
-            both = a[v, :, at : at + n].reshape(2 * n * Q, 256)
-            high = jnp.dot(both, w[m, v, 0], preferred_element_type=F32)
-            low = jnp.dot(
-                a[v, 0, at : at + n].reshape(n * Q, 256), w[m, v, 1], preferred_element_type=F32
-            )
-            new = (high[: n * Q] + high[n * Q :] + low).reshape(n, Q, 256)
+            hi, lo = (a[v, k, at : at + n].reshape(n * Q, 256) for k in range(2))
+            new = jnp.dot(
+                jnp.concatenate([hi, hi, lo], axis=1),
+                jnp.concatenate([w[m, v, 0], w[m, v, 1], w[m, v, 0]], axis=0),
+                preferred_element_type=F32,
+            ).reshape(n, Q, 256)
             acc[v, at : at + n] = new if before is None else before[v, at : at + n] + new
-        return carry
-
-    lax.fori_loop(0, 3, multiply, 0)
-
-
-def conv2_most(ids, valid, e0, o0, e1, o1, e2, o2, stats, w, acc, h, a, wbuf, sems):
-    def fetch(k):
-        return pltpu.make_async_copy(w.at[k], wbuf.at[k % 2], sems.at[k % 2])
-
-    fetch(0).start()
-    for k, pair in enumerate(((e0, o0), (e1, o1), (e2, o2))):
-        if k < 2:
-            fetch(k + 1).start()
+
+
+def conv2_near(ids, valid, e1, o1, e2, o2, stats, w, acc, w0, w3, h, a, wbuf, sems):
+    order = ((1, wbuf.at[0]), (2, wbuf.at[1]), (0, w0), (3, w3))
+    fetches = [pltpu.make_async_copy(w.at[k], to, sems.at[k]) for k, to in order]
+    for fetch in fetches:
+        fetch.start()
+    for k, pair in ((1, rows_of(e1, o1)), (2, rows_of(e2, o2))):
         norm_silu(ids, k, valid, pair, stats, h)
         fill_a(h, a)
-        fetch(k).wait()
-        multiply_second(a, wbuf.at[k % 2], acc if k else None, acc)
-
-
-def conv2_last(ids, valid, e3, o3, stats, w, before, bias, out, h, a, wbuf, sems, acc, fine):
-    fetch = pltpu.make_async_copy(w.at[3], wbuf.at[0], sems.at[0])
-    fetch.start()
-    norm_silu(ids, 3, valid, (e3, o3), stats, h)
-    fill_a(h, a)
-    fetch.wait()
-    multiply_second(a, wbuf.at[0], before, acc)
+        fetches[k - 1].wait()
+        multiply_second(a, wbuf.at[k - 1], None if k == 1 else acc, acc)
+    for fetch in fetches[2:]:
+        fetch.wait()
+
+
+def conv2_last(ids, valid, e0, o0, halo, e3, o3, stats, w0, w3, before, bias, out, h, a, acc, fine, sems):
+    plane = ids[0]
+    own = (
+        lambda t: jnp.where(plane == 3, halo[t], e0[t]),
+        lambda t: jnp.where(plane == 0, halo[t], o0[t]),
+    )
+    for k, pair, w in ((0, own, w0), (3, rows_of(e3, o3), w3)):
+        norm_silu(ids, k, valid, pair, stats, h)
+        fill_a(h, a)
+        multiply_second(a, w, before if k == 0 else acc, acc)
+    copies = []
     for half in range(2):
         lanes = slice(half * 128, half * 128 + 128)
         y = time_outputs(*(acc[0, f, :, lanes] for f in range(6)))
         for v in (1, 2):
             z = time_outputs(*(acc[v, f, :, lanes] for f in range(6)))
             for t in range(T):
-                fine[t, pl.ds(v - 1, Q, stride=2), :] = y[t] + z[t] + bias[:, lanes]
-        out[:, :, lanes] = fine[...]
+                fine[half, t, pl.ds(v - 1, Q, stride=2), :] = y[t] + z[t] + bias[:, lanes]
+        copies.append(pltpu.make_async_copy(fine.at[half], out.at[:, :, lanes], sems.at[half]))
+        copies[half].start()
+    for copy in copies:
+        copy.wait()
 
 
 SUMS = (3, 6, Q, 256)
-CONV2_SCRATCH = [
-    pltpu.VMEM((T, Q, 256), F32),
-    pltpu.VMEM((3, 2, 6, Q, 256), BF16),
-    pltpu.VMEM((2,) + W2S[1:], BF16),
-    pltpu.SemaphoreType.DMA((2,)),
-]
-
-
-def run_conv2_most(ids, valid, rows, stats, w):
-    return pl.pallas_call(
-        conv2_most,
-        in_specs=[INS, INS] + [INV] * 7 + [INH],
-        out_specs=INV,
-        scratch_shapes=CONV2_SCRATCH,
-        out_shape=jax.ShapeDtypeStruct(SUMS, F32),
+CONV2_SCRATCH = [pltpu.VMEM((T, Q, 256), F32), pltpu.VMEM((3, 2, 6, Q, 256), BF16)]
+
+
+def run_conv2_near(ids, valid, rows, stats, w):
+    block = jax.ShapeDtypeStruct(W2S[1:], BF16)
+    return pl.pallas_call(
+        conv2_near,
+        in_specs=[INS, INS] + [INV] * 5 + [INH],
+        out_specs=[INV] * 3,
+        scratch_shapes=CONV2_SCRATCH + [pltpu.VMEM((2,) + W2S[1:], BF16), pltpu.SemaphoreType.DMA((4,))],
+        out_shape=[jax.ShapeDtypeStruct(SUMS, F32), block, block],
         compiler_params=pltpu.CompilerParams(vmem_limit_bytes=14 * MB),
-        cost_estimate=pl.CostEstimate(flops=7_000_000_000, bytes_accessed=1_000_000, transcendentals=700_000),
-        name="conv2_most",
+        cost_estimate=pl.CostEstimate(flops=4_600_000_000, bytes_accessed=13_000_000, transcendentals=400_000),
+        name="conv2_near",
     )(ids, valid, *rows, stats, pltpu.with_memory_space_constraint(w, pltpu.HBM))
 
 
-def run_conv2_last(ids, valid, rows, stats, w, before, bias):
+def run_conv2_last(ids, valid, rows, stats, w0, w3, before, bias):
     return pl.pallas_call(
         conv2_last,
-        in_specs=[INS, INS] + [INV] * 3 + [INH] + [INV] * 2,
-        out_specs=INV,
-        scratch_shapes=CONV2_SCRATCH + [pltpu.VMEM(SUMS, F32), pltpu.VMEM((T, 2 * Q, 128), F32)],
-        out_shape=jax.ShapeDtypeStruct((T, 2 * Q, 256), F32),
-        compiler_params=pltpu.CompilerParams(vmem_limit_bytes=18 * MB),
-        cost_estimate=pl.CostEstimate(flops=2_300_000_000, bytes_accessed=1_000_000, transcendentals=200_000),
+        in_specs=[INS, INS] + [INV] * 10,
+        out_specs=INH,
+        scratch_shapes=CONV2_SCRATCH
+        + [pltpu.VMEM(SUMS, F32), pltpu.VMEM((2, T, 2 * Q, 128), F32), pltpu.SemaphoreType.DMA((2,))],
+        out_shape=pltpu.HBM((T, 2 * Q, 256), F32),
+        compiler_params=pltpu.CompilerParams(vmem_limit_bytes=14 * MB),
+        cost_estimate=pl.CostEstimate(flops=4_600_000_000, bytes_accessed=1_000_000, transcendentals=400_000),
         name="conv2_last",
-    )(ids, valid, *rows, stats, pltpu.with_memory_space_constraint(w, pltpu.HBM), before, bias)
+    )(ids, valid, *rows, stats, w0, w3, before, bias)
 
 
 def index(r, c):
@@ -488,20 +509,20 @@
     x, part, b, w1, w3, w0 = run_conv1_local(ids(2, 1, 3, 0), here, first_weight)
     far_lo, far_hi, x = run_conv1_edge(top, bot, x, part, b)
     got_lo, got_hi = send(far_lo, up), send(far_hi, down)
-    up_lo, up_hi, down_lo, down_hi = run_conv1_more(x, w1, w3)
+    order = ids(0, 3, 1, 2)
+    up_lo, up_hi, down_lo, down_hi, *blocks = run_conv1_near(order, x, w1, w3, second_weight)
     b1, a1 = send(up_hi, up), send(down_lo, down)
     sum_lo, sum_hi = up_lo + got_lo, down_hi + got_hi
     a2, b2 = send(sum_lo, up), send(sum_hi, down)
     own_lo, own_hi = run_conv1_more(x, w0)
 
-    order = ids(0, 3, 1, 2)
     near = jnp.where((c == 0) | (c == 3), 1, 0)
     sides = jnp.stack([c % 2, near, 1 - near]).astype(jnp.int32)
-    tied, _ = lax.optimization_barrier((second_weight, sum_hi))
-    w2 = run_prep(order, sides, tied)
+    tied = lax.optimization_barrier((*blocks, sum_hi))
+    w2 = run_prep(sides, tied[:4])
     own_lo, w2 = lax.optimization_barrier((own_lo, w2))
-    even, odd, stats = run_finish(
-        own_lo, own_hi, a1, a2, b1, b2, norm_gain[None], norm_shift[None]
+    even, odd, edge_row, stats = run_finish(
+        c[None].astype(jnp.int32), own_lo, own_hi, a1, a2, b1, b2, norm_gain[None], norm_shift[None]
     )
 
     def move(v, step, is_odd, hops):
@@ -513,8 +534,7 @@
     edge += [(index(i + 1, 3), index(i, 3)) for i in range(NR - 1)]
     stats = lax.all_to_all(stats, both, 0, 0, tiled=True).reshape(NR, NC, 4, CB)
     e2, o2 = move(e1, 1, False, 2), move(o3, -1, True, 2)
-    halo = lax.ppermute(jnp.where(c == 0, odd, even), both, edge)
-    e0, o0 = jnp.where(c == 3, halo, even), jnp.where(c == 0, halo, odd)
+    halo = lax.ppermute(edge_row, both, edge)
 
     valid = jnp.stack(
         [
@@ -522,8 +542,9 @@
             jnp.where((c == 0) & (r == 0), 0.0, 1.0),
         ]
     ).astype(F32)
-    sums = run_conv2_most(order, valid, (e0, o0, e1, o1, e3, o3), stats, w2)
-    out = run_conv2_last(order, valid, (e2, o2), stats, w2, sums, out_bias[None])
+    sums, w2_own, w2_far = run_conv2_near(order, valid, (e1, o1, e3, o3), stats, w2)
+    rows = (even, odd, halo, e2, o2)
+    out = run_conv2_last(order, valid, rows, stats, w2_own, w2_far, sums, out_bias[None])
     return out[:, None]
 
 

time: 95.9 us -> 89.8 us (0.936)
  Pallas kernels: 44.7 us -> 38.4 us
  starting transfers between devices: 39.1 us -> 40.1 us
  other arithmetic: 1.38 us -> 0.39 us
    pallas_call x2 -> x1, Pallas kernels: 10.3 us -> 3.42 us  [run_conv1_more(): pl.pallas_call(functools.partial(conv1_more, n), in_specs=[INV] * (n + 1)...]
    all_to_all x1, waiting for transfers between devices: 8.14 us -> 4.96 us  [block(): stats = lax.all_to_all(stats, both, 0, 0, tiled=True).reshape(NR, NC, 4, CB)]
    ppermute x6, waiting for transfers between devices: 0.02 us -> 2.77 us  [send(): return lax.ppermute(v, 'ch', perm)]
    ppermute x6, starting transfers between devices: 7.28 us -> 8.83 us  [move(): return lax.ppermute(v, both, row_perm(step, is_odd, hops))]
    ppermute x1, starting transfers between devices: 5.13 us -> 3.65 us  [block(): halo = lax.ppermute(edge_row, both, edge)]
    select_n x2 -> x0, other arithmetic: 1.07 us -> none  [the longest x1 1.03 us: block(): e0, o0 = (jnp.where(c == 3, halo, even), jnp.where(c == 0, halo, odd))]
    pallas_call x4 -> x5, Pallas kernels: 27.3 us -> 27.8 us  [the longest x1 7.46 us: run_conv1_near(): pl.pallas_call(conv1_near, in_specs=[INS] + [INV] * 3 + [INH], out_specs=...]
  transfers between devices with their start and end apart: 16 -> 16, of which waited for: 2 -> 3; matrix products, arithmetic and copies ran while one was open for 1% -> 0% of each run, Pallas kernels for 37% -> 31%
where the time goes in v1:
time: 89.8 us; the launch traced here: 88.8 us
  starting transfers between devices  40.1 us (45%)
  Pallas kernels  38.4 us (43%)
  waiting for transfers between devices  9.47 us (11%)
    all_to_all x1, starting transfers between devices, block(): stats = lax.all_to_all(stats, both, 0, 0, tiled=True).reshape(NR, NC, 4, CB)  12.7 us
    ppermute x6, starting transfers between devices, move(): return lax.ppermute(v, both, row_perm(step, is_odd, hops))  8.83 us
    ppermute x6, starting transfers between devices, send(): return lax.ppermute(v, 'ch', perm)  8.07 us
    pallas_call x1, Pallas kernels, run_conv1_near(): pl.pallas_call(conv1_near, in_specs=[INS] + [INV] * 3 + [INH], out_specs=...  7.46 us
    pallas_call x1, Pallas kernels, run_conv2_last(): pl.pallas_call(conv2_last, in_specs=[INS, INS] + [INV] * 10, out_specs=IN...  6.88 us
    pallas_call x1, Pallas kernels, run_prep(): pl.pallas_call(prep_second, in_specs=[INS] + [INV] * 4, out_specs=INH, sc...  6.08 us
    pallas_call x1, Pallas kernels, run_conv2_near(): pl.pallas_call(conv2_near, in_specs=[INS, INS] + [INV] * 5 + [INH], out_s...  6.03 us
    all_to_all x1, waiting for transfers between devices, block(): stats = lax.all_to_all(stats, both, 0, 0, tiled=True).reshape(NR, NC, 4, CB)  4.96 us
  transfers between devices with their start and end apart: 16, of which 3 were waited for; matrix products, arithmetic and copies ran while one was open for 0% of the time, Pallas kernels for 31%

profile of v1, /device:TPU:1, one launch (start us, length us, event | category | flops | bytes accessed | tf_op | source)
XLA Modules:
  0.0 88.8 jit_solution(2530227566357625151)
XLA Ops:
  0.0 1.3 %intake.1 = (f32[4,2,160,128]{3,2,1,0:T(8,128)S(1)}, f32[4,1,160,128]{3,2,1,0:T(8,128)S(1)}, f32[4,1,160,128]{3,2,1,0:T(8,128)S(1)}) custom-call(f32[4,2,160,128]{3,2,1,0:T(8,128)} %lat.1), custom_call_target="tpu_custom_call" | custom-call | bytes 2000000 | tf_op jit(solution)/shard_map/intake/pallas_call | solution.py:173
  1.4 4.9 %collective-permute-start = (f32[4,1,160,128]{3,2,1,0:T(8,128)S(1)}, f32[4,1,160,128]{3,2,1,0:T(8,128)S(1)}, u32[]{:S(2)}, u32[]{:S(2)}) collective-permute-start(f32[4,1,160,128]{3,2,1,0:T(8,128)S(1)} %get-tuple-element.40), channel_id=1, source_target_pairs={{0,4},{4,8},{8,12},{12,16},{16,20},{20,24},{24,28},{28,32},{32,36}... | collective-permute-start | bytes 983048 | tf_op jit(solution)/shard_map/ppermute | solution.py:497
  6.3 1.9 %collective-permute-start.1 = (f32[4,1,160,128]{3,2,1,0:T(8,128)S(1)}, f32[4,1,160,128]{3,2,1,0:T(8,128)S(1)}, u32[]{:S(2)}, u32[]{:S(2)}) collective-permute-start(f32[4,1,160,128]{3,2,1,0:T(8,128)S(1)} %get-tuple-element.41), channel_id=1, source_target_pairs={{4,0},{8,4},{12,8},{16,12},{20,16},{24,20},{28,24},{32,28},{36,32}... | collective-permute-start | bytes 983048 | tf_op jit(solution)/shard_map/ppermute | solution.py:498
  8.3 0.1 pad_add_fusion.ids
  8.3 0.1 pad_add_fusion.1.ids
  8.4 0.1 pad_add_fusion.2.sides
  8.5 4.7 %conv1_local.1 = (bf16[6,4,160,768]{3,2,1,0:T(8,128)(2,1)S(1)}, f32[6,2,160,128]{3,2,1,0:T(8,128)S(1)}, bf16[4,3,768,256]{3,2,1,0:T(8,128)(2,1)S(1)}, f32[27,128...) custom-call(s32[4]{0:T(128)S(1)} %pad_add_fusion.1.ids, ...), custom_call_target="tpu_custom_call" | custom-call | flops 3000000000 | bytes 7000000 | tf_op jit(solution)/shard_map/conv1_local/pallas_call | solution.py:187
  13.2 1.7 %collective-permute-done.1.bot = f32[4,1,160,128]{3,2,1,0:T(8,128)S(1)} collective-permute-done((f32[4,1,160,128]{3,2,1,0:T(8,128)S(1)}, f32[4,1,160,128]{3,2,1,0:T(8,128)S(1)}, u32[]{:S(2)}, u32[]{:S(2)}) %collective-permute-start.1) | collective-permute-done | bytes 327712 | tf_op jit(solution)/shard_map/ppermute | solution.py:498
  15.0 1.1 %conv1_edge.1 = (f32[2,2,160,128]{3,2,1,0:T(8,128)S(1)}, f32[2,2,160,128]{3,2,1,0:T(8,128)S(1)}, bf16[6,4,160,768]{3,2,1,0:T(8,128)(2,1)S(1)}) custom-call(f32[4,1,160,128]{3,2,1,0:T(8,128)S(1)} %collective-permute-done.top, f32[4,1,160,128]{3,2,1,0:T(8,128)S(1)} %collective-permute-done.1.bot, ...), custom_call_target="tpu_custom_call", output_to_operand_aliasing={{2}: (2, {})} | custom-call | flops 1500000000 | bytes 1000000 | tf_op jit(solution)/shard_map/conv1_edge/pallas_call | solution.py:201
  16.1 2.5 %collective-permute-start.2 = (f32[2,2,160,128]{3,2,1,0:T(8,128)S(1)}, f32[2,2,160,128]{3,2,1,0:T(8,128)S(1)}, u32[]{:S(2)}, u32[]{:S(2)}) collective-permute-start(f32[2,2,160,128]{3,2,1,0:T(8,128)S(1)} %get-tuple-element.56), channel_id=1, source_target_pairs={{1,0},{2,1},{3,2},{0,3},{5,4},{6,5},{7,6},{4,7},{9,8},{10,9},{11,1... | collective-permute-start | bytes 983048 | tf_op jit(solution)/shard_map/ppermute | solution.py:507
  18.6 7.5 %conv1_near.1 = (f32[2,2,160,128]{3,2,1,0:T(8,128)S(1)}, f32[2,2,160,128]{3,2,1,0:T(8,128)S(1)}, f32[2,2,160,128]{3,2,1,0:T(8,128)S(1)}, f32[2,2,160,128]{3,2,1,...) custom-call(s32[4]{0:T(128)S(1)} %pad_add_fusion.ids, ...), custom_call_target="tpu_custom_call" | custom-call | flops 8999999488 | bytes 16000000 | tf_op jit(solution)/shard_map/conv1_near/pallas_call | solution.py:229
  26.1 2.7 %collective-permute-start.3 = (f32[2,2,160,128]{3,2,1,0:T(8,128)S(1)}, f32[2,2,160,128]{3,2,1,0:T(8,128)S(1)}, u32[]{:S(2)}, u32[]{:S(2)}) collective-permute-start(f32[2,2,160,128]{3,2,1,0:T(8,128)S(1)} %get-tuple-element.63), channel_id=1, source_target_pairs={{1,0},{2,1},{3,2},{0,3},{5,4},{6,5},{7,6},{4,7},{9,8},{10,9},{11,1... | collective-permute-start | bytes 983048 | tf_op jit(solution)/shard_map/ppermute | solution.py:507
  28.8 2.7 %collective-permute-start.7 = (f32[2,2,160,128]{3,2,1,0:T(8,128)S(1)}, f32[2,2,160,128]{3,2,1,0:T(8,128)S(1)}, u32[]{:S(2)}, u32[]{:S(2)}) collective-permute-start(f32[2,2,160,128]{3,2,1,0:T(8,128)S(1)} %add.46), channel_id=1, source_target_pairs={{1,0},{2,1},{3,2},{0,3},{5,4},{6,5},{7,6},{4,7},{9,8},{10,9},{11,1... | collective-permute-start | bytes 983048 | tf_op jit(solution)/shard_map/ppermute | solution.py:507
  31.6 0.1 add.47
  31.6 0.1 collective-permute-start.5
  31.7 3.4 %conv1_more.1 = (f32[2,2,160,128]{3,2,1,0:T(8,128)S(1)}, f32[2,2,160,128]{3,2,1,0:T(8,128)S(1)}) custom-call(bf16[6,4,160,768]{3,2,1,0:T(8,128)(2,1)S(1)} %get-tuple-element.46.x, f32[27,128,128]{2,1,0:T(8,128)S(1)} %get-tuple-element.47.refs_0_), custom_call_target="tpu_custom_call" | custom-call | flops 4499999744 | bytes 2000000 | tf_op jit(solution)/shard_map/conv1_more/pallas_call | solution.py:216
  35.2 0.0 copy-start
  35.2 0.0 copy-start.1
  35.2 6.1 %prep_second.1.w = bf16[4,4,3,2,256,256]{5,4,3,2,1,0:T(8,128)(2,1)} custom-call(s32[3]{0:T(128)S(1)} %pad_add_fusion.2.sides, f32[27,128,256]{2,1,0:T(8,128)S(1)} %get-tuple-element.57.refs_0_, f32[27,128,256]{2,1,0:T(8,128)S(1)} %get-tuple-element.58.refs_1_, f32[27,128,256]{2,1,0:T(8,128)S(1)} %get-tuple-element.59.refs_2_, ...), custom_call_target="tpu_custom_call" | custom-call | flops 1000000 | bytes 4000000 | tf_op jit(solution)/shard_map/prep_second/pallas_call | solution.py:338
  41.3 2.8 %collective-permute-done.5.a2 = f32[2,2,160,128]{3,2,1,0:T(8,128)S(1)} collective-permute-done((f32[2,2,160,128]{3,2,1,0:T(8,128)S(1)}, f32[2,2,160,128]{3,2,1,0:T(8,128)S(1)}, u32[]{:S(2)}, u32[]{:S(2)}) %collective-permute-start.5) | collective-permute-done | bytes 327712 | tf_op jit(solution)/shard_map/ppermute | solution.py:507
  44.1 1.4 %finish_first.1 = (f32[4,160,128]{2,1,0:T(8,128)S(1)}, f32[4,160,128]{2,1,0:T(8,128)S(1)}, f32[4,160,128]{2,1,0:T(8,128)S(1)}, f32[128,4,128]{2,1,0:T(4,128)}) custom-call(s32[1]{0:T(128)} %bitcast.6.plane, f32[2,2,160,128]{3,2,1,0:T(8,128)S(1)} %get-tuple-element.61.own_lo, f32[2,2,160,128]{3,2,1,0:T(8,128)S(1)} %get-tuple-element.62.own_hi, ...), custom_call_target="tpu_custom_call" | custom-call | flops 2000000 | bytes 3000000 | tf_op jit(solution)/shard_map/finish_first/pallas_call | solution.py:273
  45.5 2.7 %collective-permute-start.11 = (f32[4,160,128]{2,1,0:T(8,128)S(1)}, f32[4,160,128]{2,1,0:T(8,128)S(1)}, u32[]{:S(2)}, u32[]{:S(2)}) collective-permute-start(f32[4,160,128]{2,1,0:T(8,128)S(1)} %get-tuple-element.68.o0), channel_id=1, source_target_pairs={{0,3},{1,4},{2,1},{3,2},{4,7},{5,8},{6,5},{7,6},{8,11},{9,12},{10,... | collective-permute-start | bytes 983048 | tf_op jit(solution)/shard_map/ppermute | solution.py:529
  48.1 2.1 %collective-permute-start.14 = (f32[4,160,128]{2,1,0:T(8,128)S(1)}, f32[4,160,128]{2,1,0:T(8,128)S(1)}, u32[]{:S(2)}, u32[]{:S(2)}) collective-permute-start(f32[4,160,128]{2,1,0:T(8,128)S(1)} %get-tuple-element.67.e0), channel_id=1, source_target_pairs={{0,127},{1,0},{2,1},{3,2},{4,3},{5,4},{6,5},{7,6},{8,7},{9,8},{10,... | collective-permute-start | bytes 983048 | tf_op jit(solution)/shard_map/ppermute | solution.py:529
  50.2 1.1 %collective-permute-start.13 = (f32[4,160,128]{2,1,0:T(8,128)S(1)}, f32[4,160,128]{2,1,0:T(8,128)S(1)}, u32[]{:S(2)}, u32[]{:S(2)}) collective-permute-start(f32[4,160,128]{2,1,0:T(8,128)S(1)} %get-tuple-element.68.o0), channel_id=1, source_target_pairs={{0,1},{1,2},{2,3},{3,4},{4,5},{5,6},{6,7},{7,8},{8,9},{9,10},{10,1... | collective-permute-start | bytes 983048 | tf_op jit(solution)/shard_map/ppermute | solution.py:529
  51.3 12.7 %all-to-all-start = ((f32[128,4,128]{2,1,0:T(4,128)}), f32[128,4,128]{2,1,0:T(4,128)S(1)}, u32[]{:S(2)}, u32[]{:S(2)}) async-start(f32[128,4,128]{2,1,0:T(4,128)} %get-tuple-element.70), calls=%async_computation | async-start | bytes 524288 | tf_op jit(solution)/shard_map/all_to_all | solution.py:535
  64.0 0.1 pad_maximum_fusion.valid
  64.1 3.6 %collective-permute-start.8 = (f32[4,160,128]{2,1,0:T(8,128)S(1)}, f32[4,160,128]{2,1,0:T(8,128)S(1)}, u32[]{:S(2)}, u32[]{:S(2)}) collective-permute-start(f32[4,160,128]{2,1,0:T(8,128)S(1)} %get-tuple-element.69), channel_id=1, source_target_pairs={{0,4},{4,8},{8,12},{12,16},{16,20},{20,24},{24,28},{28,32},{32,36}... | collective-permute-start | bytes 983048 | tf_op jit(solution)/shard_map/ppermute | solution.py:537
  67.7 0.1 collective-permute-start.10
  67.8 2.9 %collective-permute-start.12 = (f32[4,160,128]{2,1,0:T(8,128)S(1)}, f32[4,160,128]{2,1,0:T(8,128)}, u32[]{:S(2)}, u32[]{:S(2)}) collective-permute-start(f32[4,160,128]{2,1,0:T(8,128)S(1)} %collective-permute-done.11.o2), channel_id=1, source_target_pairs={{3,2},{4,3},{1,4},{2,1},{7,6},{8,7},{5,8},{6,5},{11,10},{12,11},{9... | collective-permute-start | bytes 983048 | tf_op jit(solution)/shard_map/ppermute | solution.py:529
  70.8 5.0 %all-to-all-done = f32[128,4,128]{2,1,0:T(4,128)S(1)} async-done(((f32[128,4,128]{2,1,0:T(4,128)}), f32[128,4,128]{2,1,0:T(4,128)S(1)}, u32[]{:S(2)}, u32[]{:S(2)}) %all-to-all-start) | async-done | bytes 262176 | tf_op jit(solution)/shard_map/all_to_all | solution.py:535
  75.7 6.0 %conv2_near.1 = (f32[3,6,160,256]{3,2,1,0:T(8,128)S(1)}, bf16[4,3,2,256,256]{4,3,2,1,0:T(8,128)(2,1)S(1)}, bf16[4,3,2,256,256]{4,3,2,1,0:T(8,128)(2,1)S(1)}) custom-call(s32[4]{0:T(128)S(1)} %pad_add_fusion.ids, f32[2]{0:T(128)S(1)} %pad_maximum_fusion.valid, f32[4,160,128]{2,1,0:T(8,128)S(1)} %collective-permute-done.9.e1, ...), custom_call_target="tpu_custom_call" | custom-call | flops 4600000000 | bytes 13000000 | tf_op jit(solution)/shard_map/conv2_near/pallas_call | solution.py:444
  81.8 6.9 %conv2_last.1 = f32[4,320,256]{2,1,0:T(8,128)} custom-call(s32[4]{0:T(128)S(1)} %pad_add_fusion.ids, f32[2]{0:T(128)S(1)} %pad_maximum_fusion.valid, f32[4,160,128]{2,1,0:T(8,128)S(1)} %get-tuple-element.67.e0, f32[4,160,128]{2,1,0:T(8,128)S(1)} %get-tuple-element.68.o0, f32[4,160,128]{2,1,0:T(8,128)S(1)} %collective-permute-done.8.halo, ...), custom_call_target="tpu_custom_call" | custom-call | flops 4600000000 | bytes 1000000 | tf_op jit(solution)/shard_map/conv2_last/pallas_call | solution.py:457
  (21 shorter events, 0.1 us)
Async XLA Ops:
  1.4 11.9 %collective-permute-start = (f32[4,1,160,128]{3,2,1,0:T(8,128)S(1)}, f32[4,1,160,128]{3,2,1,0:T(8,128)S(1)}, u32[]{:S(2)}, u32[]{:S(2)}) collective-permute-start(f32[4,1,160,128]{3,2,1,0:T(8,128)S(1)} %get-tuple-element.40), channel_id=1, source_target_pairs={{0,4},{4,8},{8,12},{12,16},{16,20},{20,24},{24,28},{28,32},{32,36}... | collective-permute-start | bytes 983048 | tf_op jit(solution)/shard_map/ppermute | solution.py:497
  6.3 8.7 %collective-permute-start.1 = (f32[4,1,160,128]{3,2,1,0:T(8,128)S(1)}, f32[4,1,160,128]{3,2,1,0:T(8,128)S(1)}, u32[]{:S(2)}, u32[]{:S(2)}) collective-permute-start(f32[4,1,160,128]{3,2,1,0:T(8,128)S(1)} %get-tuple-element.41), channel_id=1, source_target_pairs={{4,0},{8,4},{12,8},{16,12},{20,16},{24,20},{28,24},{32,28},{36,32}... | collective-permute-start | bytes 983048 | tf_op jit(solution)/shard_map/ppermute | solution.py:498
  16.1 12.7 %collective-permute-start.2 = (f32[2,2,160,128]{3,2,1,0:T(8,128)S(1)}, f32[2,2,160,128]{3,2,1,0:T(8,128)S(1)}, u32[]{:S(2)}, u32[]{:S(2)}) collective-permute-start(f32[2,2,160,128]{3,2,1,0:T(8,128)S(1)} %get-tuple-element.56), channel_id=1, source_target_pairs={{1,0},{2,1},{3,2},{0,3},{5,4},{6,5},{7,6},{4,7},{9,8},{10,9},{11,1... | collective-permute-start | bytes 983048 | tf_op jit(solution)/shard_map/ppermute | solution.py:507
  18.6 13.0 %collective-permute-start.4 = (f32[2,2,160,128]{3,2,1,0:T(8,128)S(1)}, f32[2,2,160,128]{3,2,1,0:T(8,128)S(1)}, u32[]{:S(2)}, u32[]{:S(2)}) collective-permute-start(f32[2,2,160,128]{3,2,1,0:T(8,128)S(1)} %get-tuple-element.65), channel_id=1, source_target_pairs={{0,1},{1,2},{2,3},{3,0},{4,5},{5,6},{6,7},{7,4},{8,9},{9,10},{10,1... | collective-permute-start | bytes 983048 | tf_op jit(solution)/shard_map/ppermute | solution.py:507
  26.1 15.2 %collective-permute-start.3 = (f32[2,2,160,128]{3,2,1,0:T(8,128)S(1)}, f32[2,2,160,128]{3,2,1,0:T(8,128)S(1)}, u32[]{:S(2)}, u32[]{:S(2)}) collective-permute-start(f32[2,2,160,128]{3,2,1,0:T(8,128)S(1)} %get-tuple-element.63), channel_id=1, source_target_pairs={{1,0},{2,1},{3,2},{0,3},{5,4},{6,5},{7,6},{4,7},{9,8},{10,9},{11,1... | collective-permute-start | bytes 983048 | tf_op jit(solution)/shard_map/ppermute | solution.py:507
  28.8 12.5 %collective-permute-start.6 = (f32[2,2,160,128]{3,2,1,0:T(8,128)S(1)}, f32[2,2,160,128]{3,2,1,0:T(8,128)S(1)}, u32[]{:S(2)}, u32[]{:S(2)}) collective-permute-start(f32[2,2,160,128]{3,2,1,0:T(8,128)S(1)} %get-tuple-element.66), channel_id=1, source_target_pairs={{0,1},{1,2},{2,3},{3,0},{4,5},{5,6},{6,7},{7,4},{8,9},{9,10},{10,1... | collective-permute-start | bytes 983048 | tf_op jit(solution)/shard_map/ppermute | solution.py:507
  28.8 12.4 %collective-permute-start.7 = (f32[2,2,160,128]{3,2,1,0:T(8,128)S(1)}, f32[2,2,160,128]{3,2,1,0:T(8,128)S(1)}, u32[]{:S(2)}, u32[]{:S(2)}) collective-permute-start(f32[2,2,160,128]{3,2,1,0:T(8,128)S(1)} %add.46), channel_id=1, source_target_pairs={{1,0},{2,1},{3,2},{0,3},{5,4},{6,5},{7,6},{4,7},{9,8},{10,9},{11,1... | collective-permute-start | bytes 983048 | tf_op jit(solution)/shard_map/ppermute | solution.py:507
  31.6 12.4 %collective-permute-start.5 = (f32[2,2,160,128]{3,2,1,0:T(8,128)S(1)}, f32[2,2,160,128]{3,2,1,0:T(8,128)S(1)}, u32[]{:S(2)}, u32[]{:S(2)}) collective-permute-start(f32[2,2,160,128]{3,2,1,0:T(8,128)S(1)} %add.47), channel_id=1, source_target_pairs={{0,1},{1,2},{2,3},{3,0},{4,5},{5,6},{6,7},{7,4},{8,9},{9,10},{10,1... | collective-permute-start | bytes 983048 | tf_op jit(solution)/shard_map/ppermute | solution.py:507
  35.2 8.9 %copy-start = (f32[128]{0:T(128)S(1)}, f32[128]{0:T(128)}, u32[]{:S(2)}) copy-start(f32[128]{0:T(128)} %param.8) | copy-start | bytes 1540
  35.2 8.9 %copy-start.1 = (f32[128]{0:T(128)S(1)}, f32[128]{0:T(128)}, u32[]{:S(2)}) copy-start(f32[128]{0:T(128)} %param.9) | copy-start | bytes 1540
  45.5 22.3 %collective-permute-start.9 = (f32[4,160,128]{2,1,0:T(8,128)S(1)}, f32[4,160,128]{2,1,0:T(8,128)S(1)}, u32[]{:S(2)}, u32[]{:S(2)}) collective-permute-start(f32[4,160,128]{2,1,0:T(8,128)S(1)} %get-tuple-element.67.e0), channel_id=1, source_target_pairs={{0,1},{1,2},{2,127},{3,0},{4,5},{5,6},{6,3},{7,4},{8,9},{9,10},{10... | collective-permute-start | bytes 983048 | tf_op jit(solution)/shard_map/ppermute | solution.py:529
  45.5 22.4 %collective-permute-start.11 = (f32[4,160,128]{2,1,0:T(8,128)S(1)}, f32[4,160,128]{2,1,0:T(8,128)S(1)}, u32[]{:S(2)}, u32[]{:S(2)}) collective-permute-start(f32[4,160,128]{2,1,0:T(8,128)S(1)} %get-tuple-element.68.o0), channel_id=1, source_target_pairs={{0,3},{1,4},{2,1},{3,2},{4,7},{5,8},{6,5},{7,6},{8,11},{9,12},{10,... | collective-permute-start | bytes 983048 | tf_op jit(solution)/shard_map/ppermute | solution.py:529
  48.1 27.6 %collective-permute-start.14 = (f32[4,160,128]{2,1,0:T(8,128)S(1)}, f32[4,160,128]{2,1,0:T(8,128)S(1)}, u32[]{:S(2)}, u32[]{:S(2)}) collective-permute-start(f32[4,160,128]{2,1,0:T(8,128)S(1)} %get-tuple-element.67.e0), channel_id=1, source_target_pairs={{0,127},{1,0},{2,1},{3,2},{4,3},{5,4},{6,5},{7,6},{8,7},{9,8},{10,... | collective-permute-start | bytes 983048 | tf_op jit(solution)/shard_map/ppermute | solution.py:529
  50.2 25.5 %collective-permute-start.13 = (f32[4,160,128]{2,1,0:T(8,128)S(1)}, f32[4,160,128]{2,1,0:T(8,128)S(1)}, u32[]{:S(2)}, u32[]{:S(2)}) collective-permute-start(f32[4,160,128]{2,1,0:T(8,128)S(1)} %get-tuple-element.68.o0), channel_id=1, source_target_pairs={{0,1},{1,2},{2,3},{3,4},{4,5},{5,6},{6,7},{7,8},{8,9},{9,10},{10,1... | collective-permute-start | bytes 983048 | tf_op jit(solution)/shard_map/ppermute | solution.py:529
  51.3 24.4 %all-to-all-start = ((f32[128,4,128]{2,1,0:T(4,128)}), f32[128,4,128]{2,1,0:T(4,128)S(1)}, u32[]{:S(2)}, u32[]{:S(2)}) async-start(f32[128,4,128]{2,1,0:T(4,128)} %get-tuple-element.70), calls=%async_computation | async-start | bytes 524288 | tf_op jit(solution)/shard_map/all_to_all | solution.py:535
  64.1 17.7 %collective-permute-start.8 = (f32[4,160,128]{2,1,0:T(8,128)S(1)}, f32[4,160,128]{2,1,0:T(8,128)S(1)}, u32[]{:S(2)}, u32[]{:S(2)}) collective-permute-start(f32[4,160,128]{2,1,0:T(8,128)S(1)} %get-tuple-element.69), channel_id=1, source_target_pairs={{0,4},{4,8},{8,12},{12,16},{16,20},{20,24},{24,28},{28,32},{32,36}... | collective-permute-start | bytes 983048 | tf_op jit(solution)/shard_map/ppermute | solution.py:537
  67.7 14.1 %collective-permute-start.10 = (f32[4,160,128]{2,1,0:T(8,128)S(1)}, f32[4,160,128]{2,1,0:T(8,128)S(1)}, u32[]{:S(2)}, u32[]{:S(2)}) collective-permute-start(f32[4,160,128]{2,1,0:T(8,128)S(1)} %collective-permute-done.9.e1), channel_id=1, source_target_pairs={{1,2},{2,127},{127,0},{0,1},{5,6},{6,3},{3,4},{4,5},{9,10},{10,7},... | collective-permute-start | bytes 983048 | tf_op jit(solution)/shard_map/ppermute | solution.py:529
  67.8 14.0 %collective-permute-start.12 = (f32[4,160,128]{2,1,0:T(8,128)S(1)}, f32[4,160,128]{2,1,0:T(8,128)}, u32[]{:S(2)}, u32[]{:S(2)}) collective-permute-start(f32[4,160,128]{2,1,0:T(8,128)S(1)} %collective-permute-done.11.o2), channel_id=1, source_target_pairs={{3,2},{4,3},{1,4},{2,1},{7,6},{8,7},{5,8},{6,5},{11,10},{12,11},{9... | collective-permute-start | bytes 983048 | tf_op jit(solution)/shard_map/ppermute | solution.py:529
  75.7 6.1 %copy-start.2 = (f32[256]{0:T(256)S(1)}, f32[256]{0:T(256)}, u32[]{:S(2)}) copy-start(f32[256]{0:T(256)} %param.11) | copy-start | bytes 3076
